TPU v7x, 512 devices: a whole 4x8x8 slice. The times are simulated.
512 devices in a mesh: dp: 2 (over core), ctx: 64 (over z, y), head: 4 (over x).
Axes of the slice: x: 4, y: 8, z: 8, core: 2. Of those that a mesh axis runs over, the one named last changes fastest.
Arguments:
- queries: bfloat16 [2, 8192, 2560], P('dp', 'ctx', 'head'), may hold values from -25 to 25
- keys: bfloat16 [2, 8192, 2560], P('dp', 'ctx', 'head'), may hold values from -25 to 25
- values: bfloat16 [2, 8192, 2560], P('dp', 'ctx', 'head'), may hold values from -6 to 6
- grad_y: bfloat16 [2, 8192, 2560], P('dp', 'ctx', 'head'), may hold values from -6 to 6
- out_gain: float32 [2560], P('head'), may hold values from 0.1 to 1.9
- offsets: int32 [2, 20], P(None, 'head'), may hold values from 0 to 63, as said below
Outputs:
- attended: bfloat16 [2, 8192, 2560], P('dp', 'ctx', 'head')
- query_grad: bfloat16 [2, 8192, 2560], P('dp', 'ctx', 'head')
- key_grad: bfloat16 [2, 8192, 2560], P('dp', 'ctx', 'head')
- value_grad: bfloat16 [2, 8192, 2560], P('dp', 'ctx', 'head')
- gain_grad: float32 [2560], P('head')
Inputs may be any that keep to these rules, and one draw needn't show every extreme that they name: Row 0 holds offsets below 8, row 1 offsets below 64.
All inputs are finite; a program needn't handle non-finite values.
Results may differ from a plain program's by a relative error of at most 0.011.
Values may be sent and summed in bfloat16 or wider, within the bound.
A program may use at most 64 MiB of HBM per device.

v0:
```python
import math
import jax
import jax.numpy as jnp
from jax import lax
from jax.sharding import PartitionSpec as P

HEAD_DIM = 128
SPAN = 4
R1 = 8
EPS = 1e-06


def swapped(block, axis, bit):
    count = lax.axis_size(axis)
    route = []
    for low in range(count):
        high = low | 1 << bit
        if high != low and high < count:
            route += [(low, high), (high, low)]
    return lax.ppermute(block, axis, route)


def pick_rows(source_rows, dilation, shifts):
    row_count, head_count, head_width = source_rows.shape
    grouped = source_rows.reshape(row_count // dilation, dilation, head_count, head_width)
    hit_mask = jnp.arange(dilation, dtype=jnp.int32).reshape(1, dilation, 1, 1) == shifts.reshape(
        1, 1, head_count, 1
    )
    chosen = jnp.where(hit_mask, grouped, jnp.zeros((), source_rows.dtype))
    return jnp.sum(chosen, axis=1, dtype=source_rows.dtype)


def place_rows(row_values, dilation, shifts):
    row_count, head_count, head_width = row_values.shape
    hit_mask = jnp.arange(dilation, dtype=jnp.int32).reshape(1, dilation, 1, 1) == shifts.reshape(
        1, 1, head_count, 1
    )
    spread = jnp.where(hit_mask, row_values[:, None], jnp.zeros((), row_values.dtype))
    return spread.reshape(row_count * dilation, head_count, head_width)


def level_scores(q_rows, k_rows):
    score_scale = 1.0 / math.sqrt(q_rows.shape[-1])
    return (
        jnp.einsum("qhe,khe->hqk", q_rows, k_rows, preferred_element_type=jnp.float32) * score_scale
    )


def attend(q_rows, k_rows, v_rows):
    scores = level_scores(q_rows, k_rows)
    row_max = jnp.max(scores, axis=-1, keepdims=True)
    log_total = row_max[..., 0] + jnp.log(jnp.sum(jnp.exp(scores - row_max), axis=-1))
    soft_rows = jnp.exp(scores - log_total[..., None]).astype(jnp.bfloat16)
    level_out = jnp.einsum("hqk,khe->qhe", soft_rows, v_rows, preferred_element_type=jnp.float32)
    return (level_out, log_total.T)


def score_grads(q_rows, k_rows, v_rows, log_total, grad_low, row_shift):
    score_scale = 1.0 / math.sqrt(q_rows.shape[-1])
    scores = level_scores(q_rows, k_rows)
    exact_soft = jnp.exp(scores - log_total.T[..., None])
    prob_grad = jnp.einsum("qhe,khe->hqk", grad_low, v_rows, preferred_element_type=jnp.float32)
    score_grad = (exact_soft * (prob_grad + row_shift.T[..., None]) * score_scale).astype(
        jnp.bfloat16
    )
    return (score_grad, exact_soft.astype(jnp.bfloat16))


def key_parts(score_grad, soft_low, q_rows, grad_low):
    k_part = jnp.einsum("hqk,qhe->khe", score_grad, q_rows, preferred_element_type=jnp.float32)
    v_part = jnp.einsum("hqk,qhe->khe", soft_low, grad_low, preferred_element_type=jnp.float32)
    return (k_part, v_part)


def query_part(score_grad, k_rows):
    return jnp.einsum("hqk,khe->qhe", score_grad, k_rows, preferred_element_type=jnp.float32)


def shards(queries, keys, values, grad_y, out_gain, offsets):
    tokens = queries.shape[1]
    flat_width = queries.shape[2]
    head_count = flat_width // HEAD_DIM
    row_shape = (tokens, head_count, HEAD_DIM)
    q_own = queries[0].reshape(row_shape)
    k_own = keys[0].reshape(row_shape)
    v_own = values[0].reshape(row_shape)
    ctx_size = lax.axis_size("ctx")
    span_bits = SPAN.bit_length() - 1
    my_place = lax.axis_index("ctx")
    mid_shift = offsets[0]
    top_shift = offsets[1]
    positions = jnp.arange(tokens, dtype=jnp.int32)
    mid_hit = (positions % R1)[:, None] == mid_shift[None, :]
    top_hit = (positions % ctx_size)[:, None] == top_shift[None, :]
    mid_q = pick_rows(q_own, R1, mid_shift)
    mid_k = pick_rows(k_own, R1, mid_shift)
    mid_v = pick_rows(v_own, R1, mid_shift)
    top_q = pick_rows(q_own, ctx_size, top_shift)
    top_k = pick_rows(k_own, ctx_size, top_shift)
    top_v = pick_rows(v_own, ctx_size, top_shift)
    mid_keys = mid_k.reshape(-1, flat_width)
    mid_vals = mid_v.reshape(-1, flat_width)
    top_keys = top_k.reshape(-1, flat_width)
    top_vals = top_v.reshape(-1, flat_width)

    def append_peer(mine, received, level_bit):
        upper_side = my_place >> level_bit & 1 == 1
        return jnp.where(
            upper_side, jnp.concatenate([received, mine], 0), jnp.concatenate([mine, received], 0)
        )

    for level_bit in range(span_bits):
        received = swapped((mid_keys, mid_vals), "ctx", level_bit)
        mid_keys = append_peer(mid_keys, received[0], level_bit)
        mid_vals = append_peer(mid_vals, received[1], level_bit)
    top_keys, top_vals = (
        lax.all_gather(top_keys, "ctx", axis=0, tiled=True),
        lax.all_gather(top_vals, "ctx", axis=0, tiled=True),
    )
    mid_keys = mid_keys.reshape(-1, head_count, HEAD_DIM)
    mid_vals = mid_vals.reshape(-1, head_count, HEAD_DIM)
    top_keys = top_keys.reshape(-1, head_count, HEAD_DIM)
    top_vals = top_vals.reshape(-1, head_count, HEAD_DIM)
    base_out, base_total = attend(q_own, k_own, v_own)
    mid_out, mid_total = attend(mid_q, mid_keys, mid_vals)
    top_out, top_total = attend(top_q, top_keys, top_vals)
    mid_full = place_rows(mid_total[..., None], R1, mid_shift)[..., 0]
    top_full = place_rows(top_total[..., None], ctx_size, top_shift)[..., 0]
    row_max = jnp.maximum(base_total, jnp.where(mid_hit, mid_full, base_total))
    row_max = jnp.maximum(row_max, jnp.where(top_hit, top_full, base_total))
    base_expo = jnp.exp(base_total - row_max)
    mid_expo = jnp.where(mid_hit, jnp.exp(mid_full - row_max), 0.0)
    top_expo = jnp.where(top_hit, jnp.exp(top_full - row_max), 0.0)
    denom = base_expo + mid_expo + top_expo
    base_share = base_expo / denom
    mid_share = mid_expo / denom
    top_share = top_expo / denom
    attn = (
        base_share[..., None] * base_out
        + mid_share[..., None] * place_rows(mid_out, R1, mid_shift)
        + top_share[..., None] * place_rows(top_out, ctx_size, top_shift)
    )
    inv_rms = lax.rsqrt(jnp.mean(attn * attn, axis=-1, keepdims=True) + EPS)
    normed = attn * inv_rms
    gain_rows = out_gain.reshape(head_count, HEAD_DIM)
    attended = (normed * gain_rows).astype(jnp.bfloat16).reshape(1, tokens, flat_width)
    grad_full = grad_y[0].reshape(row_shape).astype(jnp.float32)
    gain_part = jnp.sum(grad_full * normed, axis=0).reshape(flat_width)
    gain_grad = lax.psum(gain_part, ("dp", "ctx"))
    grad_norm = grad_full * gain_rows
    grad_attn = inv_rms * (
        grad_norm - normed * jnp.mean(grad_norm * normed, axis=-1, keepdims=True)
    )
    inner = jnp.sum(grad_attn * attn, axis=-1)
    base_low = (base_share[..., None] * grad_attn).astype(jnp.bfloat16)
    base_shift = -(base_share * inner)
    base_grad, base_soft = score_grads(q_own, k_own, v_own, base_total, base_low, base_shift)
    base_dq = query_part(base_grad, k_own)
    base_dk, base_dv = key_parts(base_grad, base_soft, q_own, base_low)
    mid_sel = pick_rows(mid_share[..., None], R1, mid_shift)[..., 0]
    mid_low = (mid_sel[..., None] * pick_rows(grad_attn, R1, mid_shift)).astype(jnp.bfloat16)
    mid_row_shift = -(mid_sel * pick_rows(inner[..., None], R1, mid_shift)[..., 0])
    mid_grad, mid_soft = score_grads(mid_q, mid_keys, mid_vals, mid_total, mid_low, mid_row_shift)
    mid_dq = query_part(mid_grad, mid_keys)
    mid_dk, mid_dv = key_parts(mid_grad, mid_soft, mid_q, mid_low)
    mid_dk = mid_dk.reshape(-1, flat_width)
    mid_dv = mid_dv.reshape(-1, flat_width)
    for level_bit in reversed(range(span_bits)):
        half_rows = mid_dk.shape[0] // 2
        upper_side = my_place >> level_bit & 1 == 1
        keep_k = jnp.where(upper_side, mid_dk[half_rows:], mid_dk[:half_rows])
        keep_v = jnp.where(upper_side, mid_dv[half_rows:], mid_dv[:half_rows])
        send_k = jnp.where(upper_side, mid_dk[:half_rows], mid_dk[half_rows:])
        send_v = jnp.where(upper_side, mid_dv[:half_rows], mid_dv[half_rows:])
        received = (
            swapped(send_k.astype(jnp.bfloat16), "ctx", level_bit).astype(send_k.dtype),
            swapped(send_v.astype(jnp.bfloat16), "ctx", level_bit).astype(send_v.dtype),
        )
        mid_dk = keep_k + received[0]
        mid_dv = keep_v + received[1]
    mid_dk = mid_dk.reshape(-1, head_count, HEAD_DIM)
    mid_dv = mid_dv.reshape(-1, head_count, HEAD_DIM)
    top_sel = pick_rows(top_share[..., None], ctx_size, top_shift)[..., 0]
    top_low = (top_sel[..., None] * pick_rows(grad_attn, ctx_size, top_shift)).astype(jnp.bfloat16)
    top_row_shift = -(top_sel * pick_rows(inner[..., None], ctx_size, top_shift)[..., 0])
    top_grad, top_soft = score_grads(top_q, top_keys, top_vals, top_total, top_low, top_row_shift)
    top_dq = query_part(top_grad, top_keys)
    gathered_dk, gathered_dv = key_parts(top_grad, top_soft, top_q, top_low)
    summed = (
        lax.psum_scatter(
            gathered_dk.reshape(-1, flat_width), "ctx", scatter_dimension=0, tiled=True
        ),
        lax.psum_scatter(
            gathered_dv.reshape(-1, flat_width), "ctx", scatter_dimension=0, tiled=True
        ),
    )
    top_dk = summed[0].reshape(-1, head_count, HEAD_DIM)
    top_dv = summed[1].reshape(-1, head_count, HEAD_DIM)
    query_grad = (
        base_dq + place_rows(mid_dq, R1, mid_shift) + place_rows(top_dq, ctx_size, top_shift)
    )
    key_grad = base_dk + place_rows(mid_dk, R1, mid_shift) + place_rows(top_dk, ctx_size, top_shift)
    value_grad = (
        base_dv + place_rows(mid_dv, R1, mid_shift) + place_rows(top_dv, ctx_size, top_shift)
    )
    out_shape = (1, tokens, flat_width)
    return (
        attended,
        query_grad.astype(jnp.bfloat16).reshape(out_shape),
        key_grad.astype(jnp.bfloat16).reshape(out_shape),
        value_grad.astype(jnp.bfloat16).reshape(out_shape),
        gain_grad,
    )


def solution(mesh):
    in_specs = (
        P("dp", "ctx", "head"),
        P("dp", "ctx", "head"),
        P("dp", "ctx", "head"),
        P("dp", "ctx", "head"),
        P("head"),
        P(None, "head"),
    )
    out_specs = (
        P("dp", "ctx", "head"),
        P("dp", "ctx", "head"),
        P("dp", "ctx", "head"),
        P("dp", "ctx", "head"),
        P("head"),
    )
    return jax.shard_map(shards, mesh=mesh, in_specs=in_specs, out_specs=out_specs, check_vma=False)
```

profile of v0, /device:TPU:266, one launch (start us, length us, event | category | flops | bytes accessed | tf_op | source)
XLA Modules:
  0.0 443.0 jit_solution(7934693849912801585)
XLA Ops:
  7.2 0.8 slice_bitcast_fusion.1
  8.0 1.5 fusion.26
  9.6 2.4 collective-permute-start
  12.0 3.6 collective-permute-start.2
  15.6 0.2 copy.143
  15.8 0.2 copy.144
  15.9 0.2 reshape_reshape_squeeze.20
  16.2 0.2 reshape_reshape_squeeze.21
  16.4 0.7 copy-done.2
  17.1 0.2 reshape_reshape_squeeze.23
  17.5 0.3 select_reduce_fusion
  17.8 48.5 %all-gather = bf16[64,2,640]{2,1,0:T(2,128)(2,1)S(1)} all-gather(bf16[1,2,640]{2,1,0:T(2,128)(2,1)S(1)} %reshape.367), channel_id=1, replica_groups=mesh['dp'=2,'ctx'=64,'head'=4] {'ctx'}, dimensions={0}, use_global_device_ids=true | all-gather | bytes 166400 | tf_op jit(solution)/shard_map/all_gather | solution.py:117
  66.4 0.3 fusion.58
  66.7 0.2 exponential_reduce_fusion.2
  67.0 47.4 %all-gather.1 = bf16[64,2,640]{2,1,0:T(2,128)(2,1)S(1)} all-gather(bf16[1,2,640]{2,1,0:T(2,128)(2,1)S(1)} %reshape.369), channel_id=1, replica_groups=mesh['dp'=2,'ctx'=64,'head'=4] {'ctx'}, dimensions={0}, use_global_device_ids=true | all-gather | bytes 166400 | tf_op jit(solution)/shard_map/all_gather | solution.py:118
  114.4 0.2 convolution_bitcast_fusion.9
  114.6 0.3 fusion.60
  115.0 0.2 copy.157
  115.4 0.5 copy-done.4
  115.9 0.2 copy.168
  116.1 0.2 copy.169
  116.4 1.3 dynamic-slice
  118.4 4.6 %collective-permute-start.1 = (bf16[32,640]{1,0:T(8,128)(2,1)S(1)}, bf16[32,640]{1,0:T(8,128)(2,1)S(1)}, u32[]{:S(2)}, u32[]{:S(2)}) collective-permute-start(bf16[32,640]{1,0:T(8,128)(2,1)S(1)} %maximum_select_fusion.2), channel_id=1, source_target_pairs={{0,8},{8,0},{4,12},{12,4},{16,24},{24,16},{20,28},{28,20},{32,40},... | collective-permute-start | bytes 122888 | tf_op jit(solution)/shard_map/ppermute | solution.py:20
  123.0 2.2 collective-permute-start.3
  125.3 0.2 fusion.59
  125.5 0.2 exponential_reduce_fusion.1
  126.2 0.2 fusion.23
  126.4 3.4 collective-permute-done.3
  129.8 0.2 convolution_bitcast_fusion.7
  130.0 0.5 multiply_reduce_fusion.3
  130.6 0.7 copy-done.5
  131.2 0.3 multiply_reduce_fusion
  131.5 0.3 fusion.22
  131.8 0.2 multiply_reduce_fusion.1
  132.1 0.2 fusion.21
  132.7 0.2 fusion.20
  132.9 0.2 convolution_bitcast_fusion.8
  133.0 1.0 fusion.50
  134.1 1.0 fusion.47
  135.1 0.4 fusion.14
  135.6 0.3 convolution_bitcast_fusion.4
  135.9 0.2 fusion.17
  136.1 2.2 collective-permute-start.6
  138.3 0.2 convolution_bitcast_fusion.5
  138.7 4.6 %collective-permute-start.4 = (bf16[32,640]{1,0:T(8,128)(2,1)S(1)}, bf16[32,640]{1,0:T(8,128)(2,1)S(1)}, u32[]{:S(2)}, u32[]{:S(2)}) collective-permute-start(bf16[32,640]{1,0:T(8,128)(2,1)S(1)} %copy_bitcast_fusion.1), channel_id=1, source_target_pairs={{0,8},{8,0},{4,12},{12,4},{16,24},{24,16},{20,28},{28,20},{32,40},... | collective-permute-start | bytes 122888 | tf_op jit(solution)/shard_map/ppermute | solution.py:20
  143.3 0.2 copy.167
  143.4 0.8 copy.198
  144.3 275.7 %psum.7 = f32[640]{0:T(1024)} all-reduce(f32[640]{0:T(1024)S(1)} %bitcast.253), channel_id=1, replica_groups=mesh['dp'=2,'ctx'=64,'head'=4] {'dp','ctx'}, use_global_device_ids=true, to_apply=%region_24.25 | all-reduce | flops 640 | bytes 5120 | tf_op jit(solution)/shard_map/psum | solution.py:149
  420.0 4.7 %collective-permute-start.7 = (bf16[16,640]{1,0:T(8,128)(2,1)S(1)}, bf16[16,640]{1,0:T(8,128)(2,1)S(1)}, u32[]{:S(2)}, u32[]{:S(2)}) collective-permute-start(bf16[16,640]{1,0:T(8,128)(2,1)S(1)} %select_convert_fusion.2), channel_id=1, source_target_pairs={{0,4},{4,0},{8,12},{12,8},{16,20},{20,16},{24,28},{28,24},{32,36},... | collective-permute-start | bytes 61448 | tf_op jit(solution)/shard_map/ppermute | solution.py:20
  424.8 1.9 collective-permute-start.5
  426.8 3.7 collective-permute-done.5
  430.6 1.2 constant_dynamic-slice_fusion.1
  431.8 0.1 constant_dynamic-slice_fusion
  432.0 0.2 copy.186
  432.2 0.2 bitcast_select_fusion
  432.4 0.2 fusion.12
  432.6 0.2 copy.187
  432.8 0.8 copy.200
  433.6 0.3 fusion.11
  433.9 0.2 copy.179
  434.1 0.8 copy.199
  434.9 0.3 fusion.13
  435.2 0.2 copy.196
  435.4 0.8 copy.201
  (73 shorter events, 2.7 us)
Async XLA Ops:
  7.2 423.4 %all-reduce.5.cloned.1.call-start = ((), (), s32[]{:S(2)}) async-start(), calls=%async_computation | async-start | bytes 1310720
  8.0 7.6 %copy-start = (bf16[1,128,640]{2,1,0:T(8,128)(2,1)S(1)}, bf16[1,128,640]{2,1,0:T(8,128)(2,1)}, u32[]{:S(2)}) copy-start(bf16[1,128,640]{2,1,0:T(8,128)(2,1)} %param.6) | copy-start | bytes 491524
  9.6 108.7 %collective-permute-start = (bf16[16,640]{1,0:T(8,128)(2,1)S(1)}, bf16[16,640]{1,0:T(8,128)(2,1)S(1)}, u32[]{:S(2)}, u32[]{:S(2)}) collective-permute-start(bf16[16,640]{1,0:T(8,128)(2,1)S(1)} %copy_bitcast_fusion.7), channel_id=1, source_target_pairs={{0,4},{4,0},{8,12},{12,8},{16,20},{20,16},{24,28},{28,24},{32,36},... | collective-permute-start | bytes 61448 | tf_op jit(solution)/shard_map/ppermute | solution.py:20
  12.0 3.8 copy-start.1
  12.0 106.4 %collective-permute-start.2 = (bf16[16,640]{1,0:T(8,128)(2,1)S(1)}, bf16[16,640]{1,0:T(8,128)(2,1)S(1)}, u32[]{:S(2)}, u32[]{:S(2)}) collective-permute-start(bf16[16,640]{1,0:T(8,128)(2,1)S(1)} %copy_bitcast_fusion.6), channel_id=1, source_target_pairs={{0,4},{4,0},{8,12},{12,8},{16,20},{20,16},{24,28},{28,24},{32,36},... | collective-permute-start | bytes 61448 | tf_op jit(solution)/shard_map/ppermute | solution.py:20
  16.2 0.9 copy-start.2
  115.0 0.9 copy-start.4
  118.4 6.9 %collective-permute-start.1 = (bf16[32,640]{1,0:T(8,128)(2,1)S(1)}, bf16[32,640]{1,0:T(8,128)(2,1)S(1)}, u32[]{:S(2)}, u32[]{:S(2)}) collective-permute-start(bf16[32,640]{1,0:T(8,128)(2,1)S(1)} %maximum_select_fusion.2), channel_id=1, source_target_pairs={{0,8},{8,0},{4,12},{12,4},{16,24},{24,16},{20,28},{28,20},{32,40},... | collective-permute-start | bytes 122888 | tf_op jit(solution)/shard_map/ppermute | solution.py:20
  123.0 6.8 %collective-permute-start.3 = (bf16[32,640]{1,0:T(8,128)(2,1)S(1)}, bf16[32,640]{1,0:T(8,128)(2,1)S(1)}, u32[]{:S(2)}, u32[]{:S(2)}) collective-permute-start(bf16[32,640]{1,0:T(8,128)(2,1)S(1)} %maximum_select_fusion.4), channel_id=1, source_target_pairs={{0,8},{8,0},{4,12},{12,4},{16,24},{24,16},{20,28},{28,20},{32,40},... | collective-permute-start | bytes 122888 | tf_op jit(solution)/shard_map/ppermute | solution.py:20
  130.5 0.7 copy-start.5
  136.1 283.9 %collective-permute-start.6 = (bf16[32,640]{1,0:T(8,128)(2,1)S(1)}, bf16[32,640]{1,0:T(8,128)(2,1)S(1)}, u32[]{:S(2)}, u32[]{:S(2)}) collective-permute-start(bf16[32,640]{1,0:T(8,128)(2,1)S(1)} %copy_bitcast_fusion), channel_id=1, source_target_pairs={{0,8},{8,0},{4,12},{12,4},{16,24},{24,16},{20,28},{28,20},{32,40},... | collective-permute-start | bytes 122888 | tf_op jit(solution)/shard_map/ppermute | solution.py:20
  138.7 286.1 %collective-permute-start.4 = (bf16[32,640]{1,0:T(8,128)(2,1)S(1)}, bf16[32,640]{1,0:T(8,128)(2,1)S(1)}, u32[]{:S(2)}, u32[]{:S(2)}) collective-permute-start(bf16[32,640]{1,0:T(8,128)(2,1)S(1)} %copy_bitcast_fusion.1), channel_id=1, source_target_pairs={{0,8},{8,0},{4,12},{12,4},{16,24},{24,16},{20,28},{28,20},{32,40},... | collective-permute-start | bytes 122888 | tf_op jit(solution)/shard_map/ppermute | solution.py:20
  420.0 6.7 %collective-permute-start.7 = (bf16[16,640]{1,0:T(8,128)(2,1)S(1)}, bf16[16,640]{1,0:T(8,128)(2,1)S(1)}, u32[]{:S(2)}, u32[]{:S(2)}) collective-permute-start(bf16[16,640]{1,0:T(8,128)(2,1)S(1)} %select_convert_fusion.2), channel_id=1, source_target_pairs={{0,4},{4,0},{8,12},{12,8},{16,20},{20,16},{24,28},{28,24},{32,36},... | collective-permute-start | bytes 61448 | tf_op jit(solution)/shard_map/ppermute | solution.py:20
  424.8 5.7 %collective-permute-start.5 = (bf16[16,640]{1,0:T(8,128)(2,1)S(1)}, bf16[16,640]{1,0:T(8,128)(2,1)S(1)}, u32[]{:S(2)}, u32[]{:S(2)}) collective-permute-start(bf16[16,640]{1,0:T(8,128)(2,1)S(1)} %select_convert_fusion.3), channel_id=1, source_target_pairs={{0,4},{4,0},{8,12},{12,8},{16,20},{20,16},{24,28},{28,24},{32,36},... | collective-permute-start | bytes 61448 | tf_op jit(solution)/shard_map/ppermute | solution.py:20
  430.6 1.2 copy-start.3
Sparse Core Ops, SparseCore 0:
  144.4 154.0 all-reduce.4
where the time goes:
time: 444 us; the launch traced here: 443 us
  blocking collectives  372 us (84%)
  starting transfers between devices  26.2 us (6%)
  between operations  15.2 us (3%)
  local copies, waits for them, and re-layouts  12.3 us (3%)
  waiting for transfers between devices  7.26 us (2%)
  matrix products  6.13 us (1%)
    psum x1, blocking collectives, shards(): gain_grad = lax.psum(gain_part, ('dp', 'ctx'))  276 us
    all_gather x1, blocking collectives, shards(): lax.all_gather(top_keys, 'ctx', axis=0, tiled=True)  48.5 us
    all_gather x1, blocking collectives, shards(): lax.all_gather(top_vals, 'ctx', axis=0, tiled=True)  47.4 us
    ppermute x8, starting transfers between devices, swapped(): return lax.ppermute(block, axis, route)  26.1 us
  transfers between devices with their start and end apart: 9, of which 3 were waited for; matrix products, arithmetic and copies ran while one was open for 2% of the time, Pallas kernels for 0%

commit v1 on v0

--- a/solution.py
+++ b/solution.py
@@ -146,7 +146,7 @@
     attended = (normed * gain_rows).astype(jnp.bfloat16).reshape(1, tokens, flat_width)
     grad_full = grad_y[0].reshape(row_shape).astype(jnp.float32)
     gain_part = jnp.sum(grad_full * normed, axis=0).reshape(flat_width)
-    gain_grad = lax.psum(gain_part, ("dp", "ctx"))
+    gain_grad = lax.psum(lax.psum(gain_part, "dp"), "ctx")
     grad_norm = grad_full * gain_rows
     grad_attn = inv_rms * (
         grad_norm - normed * jnp.mean(grad_norm * normed, axis=-1, keepdims=True)

time: 444 us -> 317 us (0.71)
  the two profiles are of different devices: /device:TPU:266 before, /device:TPU:2 now
where the time goes in v1:
time: 317 us
  blocking collectives  248 us (78%)
  starting transfers between devices  25.3 us (8%)
  between operations  15.2 us (5%)
  local copies, waits for them, and re-layouts  12.3 us (4%)
  matrix products  6.13 us (2%)
  waiting for transfers between devices  5.28 us (2%)
  other arithmetic  4.4 us (1%)
    psum x2, blocking collectives, shards(): gain_grad = lax.psum(lax.psum(gain_part, 'dp'), 'ctx')  144 us
    all_gather x1, blocking collectives, shards(): lax.all_gather(top_keys, 'ctx', axis=0, tiled=True)  56.5 us
    all_gather x1, blocking collectives, shards(): lax.all_gather(top_vals, 'ctx', axis=0, tiled=True)  47.7 us
    ppermute x8, starting transfers between devices, swapped(): return lax.ppermute(block, axis, route)  25.3 us
    unnamed x25, local copies, waits for them, and re-layouts  8.48 us
  transfers between devices with their start and end apart: 9, of which 4 were waited for; matrix products, arithmetic and copies ran while one was open for 2% of the time, Pallas kernels for 0%

profile of v1, /device:TPU:2, one launch (start us, length us, event | category | flops | bytes accessed | tf_op | source)
XLA Modules:
  0.0 316.6 jit_solution(4228230237603019472)
XLA Ops:
  7.2 0.8 slice_bitcast_fusion.1
  8.0 1.5 fusion.26
  9.6 3.5 %collective-permute-start = (bf16[16,640]{1,0:T(8,128)(2,1)S(1)}, bf16[16,640]{1,0:T(8,128)(2,1)S(1)}, u32[]{:S(2)}, u32[]{:S(2)}) collective-permute-start(bf16[16,640]{1,0:T(8,128)(2,1)S(1)} %copy_bitcast_fusion.7), channel_id=1, source_target_pairs={{0,4},{4,0},{8,12},{12,8},{16,20},{20,16},{24,28},{28,24},{32,36},... | collective-permute-start | bytes 61448 | tf_op jit(solution)/shard_map/ppermute | solution.py:20
  13.1 2.5 collective-permute-start.2
  15.6 0.2 copy.143
  15.8 0.2 copy.144
  15.9 0.2 reshape_reshape_squeeze.20
  16.2 0.2 reshape_reshape_squeeze.21
  16.4 0.7 copy-done.2
  17.1 0.2 reshape_reshape_squeeze.23
  17.5 0.3 select_reduce_fusion
  17.8 56.5 %all-gather = bf16[64,2,640]{2,1,0:T(2,128)(2,1)S(1)} all-gather(bf16[1,2,640]{2,1,0:T(2,128)(2,1)S(1)} %reshape.367), channel_id=1, replica_groups=mesh['dp'=2,'ctx'=64,'head'=4] {'ctx'}, dimensions={0}, use_global_device_ids=true | all-gather | bytes 166400 | tf_op jit(solution)/shard_map/all_gather | solution.py:117
  74.4 0.3 fusion.58
  74.7 0.2 exponential_reduce_fusion.2
  75.0 47.7 %all-gather.1 = bf16[64,2,640]{2,1,0:T(2,128)(2,1)S(1)} all-gather(bf16[1,2,640]{2,1,0:T(2,128)(2,1)S(1)} %reshape.369), channel_id=1, replica_groups=mesh['dp'=2,'ctx'=64,'head'=4] {'ctx'}, dimensions={0}, use_global_device_ids=true | all-gather | bytes 166400 | tf_op jit(solution)/shard_map/all_gather | solution.py:118
  122.8 0.2 convolution_bitcast_fusion.9
  122.9 0.3 fusion.60
  123.3 0.2 copy.157
  123.7 0.5 copy-done.4
  124.2 0.2 copy.168
  124.7 1.3 dynamic-slice
  126.7 2.7 collective-permute-start.1
  129.5 4.0 %collective-permute-start.3 = (bf16[32,640]{1,0:T(8,128)(2,1)S(1)}, bf16[32,640]{1,0:T(8,128)(2,1)S(1)}, u32[]{:S(2)}, u32[]{:S(2)}) collective-permute-start(bf16[32,640]{1,0:T(8,128)(2,1)S(1)} %maximum_select_fusion.4), channel_id=1, source_target_pairs={{0,8},{8,0},{4,12},{12,4},{16,24},{24,16},{20,28},{28,20},{32,40},... | collective-permute-start | bytes 122888 | tf_op jit(solution)/shard_map/ppermute | solution.py:20
  133.5 0.5 collective-permute-done.1
  134.0 0.2 fusion.59
  134.2 0.2 exponential_reduce_fusion.1
  134.8 0.2 fusion.23
  135.1 1.2 collective-permute-done.3
  136.3 0.2 convolution_bitcast_fusion.7
  136.5 0.5 multiply_reduce_fusion.3
  137.0 0.7 copy-done.5
  137.7 0.3 multiply_reduce_fusion
  138.0 0.3 fusion.22
  138.3 0.2 multiply_reduce_fusion.1
  138.6 0.2 fusion.21
  139.2 0.2 fusion.20
  139.4 0.2 convolution_bitcast_fusion.8
  139.5 1.0 fusion.50
  140.5 1.0 fusion.47
  141.5 0.4 fusion.14
  142.0 0.3 convolution_bitcast_fusion.4
  142.4 0.2 fusion.17
  142.6 4.0 %collective-permute-start.6 = (bf16[32,640]{1,0:T(8,128)(2,1)S(1)}, bf16[32,640]{1,0:T(8,128)(2,1)S(1)}, u32[]{:S(2)}, u32[]{:S(2)}) collective-permute-start(bf16[32,640]{1,0:T(8,128)(2,1)S(1)} %copy_bitcast_fusion), channel_id=1, source_target_pairs={{0,8},{8,0},{4,12},{12,4},{16,24},{24,16},{20,28},{28,20},{32,40},... | collective-permute-start | bytes 122888 | tf_op jit(solution)/shard_map/ppermute | solution.py:20
  146.6 0.2 convolution_bitcast_fusion.5
  147.0 2.7 collective-permute-start.4
  149.8 0.2 copy.167
  149.9 0.8 copy.198
  150.8 2.5 psum.14
  153.2 141.3 %psum.15 = f32[640]{0:T(1024)} all-reduce(f32[640]{0:T(1024)S(1)} %psum.14), channel_id=1, replica_groups=mesh['dp'=2,'ctx'=64,'head'=4] {'ctx'}, use_global_device_ids=true, to_apply=%region_25.26 | all-reduce | flops 640 | bytes 5120 | tf_op jit(solution)/shard_map/psum | solution.py:149
  294.6 1.9 collective-permute-start.7
  296.5 3.9 %collective-permute-start.5 = (bf16[16,640]{1,0:T(8,128)(2,1)S(1)}, bf16[16,640]{1,0:T(8,128)(2,1)S(1)}, u32[]{:S(2)}, u32[]{:S(2)}) collective-permute-start(bf16[16,640]{1,0:T(8,128)(2,1)S(1)} %select_convert_fusion.3), channel_id=1, source_target_pairs={{0,4},{4,0},{8,12},{12,8},{16,20},{20,16},{24,28},{28,24},{32,36},... | collective-permute-start | bytes 61448 | tf_op jit(solution)/shard_map/ppermute | solution.py:20
  300.5 1.8 collective-permute-done.5
  302.3 1.8 all-reduce.5.cloned.1.call-done
  304.1 1.2 constant_dynamic-slice_fusion.1
  305.7 0.2 bitcast_select_fusion
  305.9 0.2 fusion.12
  306.2 0.2 copy.187
  306.3 0.8 copy.200
  307.2 0.3 fusion.11
  307.4 0.2 copy.179
  307.6 0.8 copy.199
  308.4 0.3 fusion.13
  308.7 0.2 copy.196
  308.9 0.8 copy.201
  (74 shorter events, 3.0 us)
Async XLA Ops:
  7.2 296.9 %all-reduce.5.cloned.1.call-start = ((), (), s32[]{:S(2)}) async-start(), calls=%async_computation | async-start | bytes 1310720
  8.0 7.6 %copy-start = (bf16[1,128,640]{2,1,0:T(8,128)(2,1)S(1)}, bf16[1,128,640]{2,1,0:T(8,128)(2,1)}, u32[]{:S(2)}) copy-start(bf16[1,128,640]{2,1,0:T(8,128)(2,1)} %param.6) | copy-start | bytes 491524
  9.6 117.0 %collective-permute-start = (bf16[16,640]{1,0:T(8,128)(2,1)S(1)}, bf16[16,640]{1,0:T(8,128)(2,1)S(1)}, u32[]{:S(2)}, u32[]{:S(2)}) collective-permute-start(bf16[16,640]{1,0:T(8,128)(2,1)S(1)} %copy_bitcast_fusion.7), channel_id=1, source_target_pairs={{0,4},{4,0},{8,12},{12,8},{16,20},{20,16},{24,28},{28,24},{32,36},... | collective-permute-start | bytes 61448 | tf_op jit(solution)/shard_map/ppermute | solution.py:20
  13.1 2.7 copy-start.1
  13.1 113.6 %collective-permute-start.2 = (bf16[16,640]{1,0:T(8,128)(2,1)S(1)}, bf16[16,640]{1,0:T(8,128)(2,1)S(1)}, u32[]{:S(2)}, u32[]{:S(2)}) collective-permute-start(bf16[16,640]{1,0:T(8,128)(2,1)S(1)} %copy_bitcast_fusion.6), channel_id=1, source_target_pairs={{0,4},{4,0},{8,12},{12,8},{16,20},{20,16},{24,28},{28,24},{32,36},... | collective-permute-start | bytes 61448 | tf_op jit(solution)/shard_map/ppermute | solution.py:20
  16.2 0.9 copy-start.2
  123.3 0.9 copy-start.4
  126.7 7.2 %collective-permute-start.1 = (bf16[32,640]{1,0:T(8,128)(2,1)S(1)}, bf16[32,640]{1,0:T(8,128)(2,1)S(1)}, u32[]{:S(2)}, u32[]{:S(2)}) collective-permute-start(bf16[32,640]{1,0:T(8,128)(2,1)S(1)} %maximum_select_fusion.2), channel_id=1, source_target_pairs={{0,8},{8,0},{4,12},{12,4},{16,24},{24,16},{20,28},{28,20},{32,40},... | collective-permute-start | bytes 122888 | tf_op jit(solution)/shard_map/ppermute | solution.py:20
  129.5 6.8 %collective-permute-start.3 = (bf16[32,640]{1,0:T(8,128)(2,1)S(1)}, bf16[32,640]{1,0:T(8,128)(2,1)S(1)}, u32[]{:S(2)}, u32[]{:S(2)}) collective-permute-start(bf16[32,640]{1,0:T(8,128)(2,1)S(1)} %maximum_select_fusion.4), channel_id=1, source_target_pairs={{0,8},{8,0},{4,12},{12,4},{16,24},{24,16},{20,28},{28,20},{32,40},... | collective-permute-start | bytes 122888 | tf_op jit(solution)/shard_map/ppermute | solution.py:20
  137.0 0.7 copy-start.5
  142.6 151.9 %collective-permute-start.6 = (bf16[32,640]{1,0:T(8,128)(2,1)S(1)}, bf16[32,640]{1,0:T(8,128)(2,1)S(1)}, u32[]{:S(2)}, u32[]{:S(2)}) collective-permute-start(bf16[32,640]{1,0:T(8,128)(2,1)S(1)} %copy_bitcast_fusion), channel_id=1, source_target_pairs={{0,8},{8,0},{4,12},{12,4},{16,24},{24,16},{20,28},{28,20},{32,40},... | collective-permute-start | bytes 122888 | tf_op jit(solution)/shard_map/ppermute | solution.py:20
  147.0 149.5 %collective-permute-start.4 = (bf16[32,640]{1,0:T(8,128)(2,1)S(1)}, bf16[32,640]{1,0:T(8,128)(2,1)S(1)}, u32[]{:S(2)}, u32[]{:S(2)}) collective-permute-start(bf16[32,640]{1,0:T(8,128)(2,1)S(1)} %copy_bitcast_fusion.1), channel_id=1, source_target_pairs={{0,8},{8,0},{4,12},{12,4},{16,24},{24,16},{20,28},{28,20},{32,40},... | collective-permute-start | bytes 122888 | tf_op jit(solution)/shard_map/ppermute | solution.py:20
  294.6 5.9 %collective-permute-start.7 = (bf16[16,640]{1,0:T(8,128)(2,1)S(1)}, bf16[16,640]{1,0:T(8,128)(2,1)S(1)}, u32[]{:S(2)}, u32[]{:S(2)}) collective-permute-start(bf16[16,640]{1,0:T(8,128)(2,1)S(1)} %select_convert_fusion.2), channel_id=1, source_target_pairs={{0,4},{4,0},{8,12},{12,8},{16,20},{20,16},{24,28},{28,24},{32,36},... | collective-permute-start | bytes 61448 | tf_op jit(solution)/shard_map/ppermute | solution.py:20
  296.5 5.7 %collective-permute-start.5 = (bf16[16,640]{1,0:T(8,128)(2,1)S(1)}, bf16[16,640]{1,0:T(8,128)(2,1)S(1)}, u32[]{:S(2)}, u32[]{:S(2)}) collective-permute-start(bf16[16,640]{1,0:T(8,128)(2,1)S(1)} %select_convert_fusion.3), channel_id=1, source_target_pairs={{0,4},{4,0},{8,12},{12,8},{16,20},{20,16},{24,28},{28,24},{32,36},... | collective-permute-start | bytes 61448 | tf_op jit(solution)/shard_map/ppermute | solution.py:20
  304.1 1.2 copy-start.3
Sparse Core Ops, SparseCore 0:
  150.9 153.1 all-reduce.4
